TPU v7x, 32 devices: a whole 2x2x4 slice. The times are simulated.
32 devices in a mesh: parts: 2 (over y), ep: 4 (over z), fs: 4 (over x, core).
Axes of the slice: x: 2, y: 2, z: 4, core: 2. Of those that a mesh axis runs over, the one named last changes fastest.
Arguments:
- hidden_states: bfloat16 [8, 512, 1152], P(('parts', 'fs'), 'ep'), parts along dimension 0, may hold values from -6 to 6
- expert_ids: int32 [8, 512, 2], P(('parts', 'fs'), 'ep'), parts along dimension 0, may hold values from 0 to 15, all different within a row; in each aligned block of 128 rows (0 to 127, 128 to 255, ..., all dimensions but the last counted through in order) at most 20 rows name the same one
- modulation: float32 [8, 3, 1152], P(('parts', 'fs')), parts along dimension 0, may hold values from -4 to 4
- router_weight: bfloat16 [1152, 16], replicated, may hold values from -0.1875 to 0.1875
- w_in: bfloat16 [32, 1152, 2304], P('ep', 'fs'), may hold values from -0.1875 to 0.1875
- b_in: float32 [32, 2304], P('ep'), may hold values from -3 to 3
- w_out: bfloat16 [32, 2304, 1152], P('ep', 'fs'), may hold values from -0.09375 to 0.09375
Outputs:
- layer_out: bfloat16 [8, 512, 1152], P(('parts', 'fs'), 'ep'), parts along dimension 0
There are 2 independent parts, one for each index of `parts`. A program takes and returns all parts, laid end to end along the dimension named above; an argument that names none is the same for every part. Nothing has to cross between parts.
Inputs may be any that keep to these rules, and one draw needn't show every extreme that they name: `expert_ids`: the two ids of a token differ. In each aligned block of 128 tokens of an image, no expert is named by more than 20 tokens, a bound that some block reaches.
All inputs are finite; a program needn't handle non-finite values.
Results may differ from a plain program's by a relative error of at most 0.0046.
Values may be sent and summed in bfloat16 or wider, within the bound.
A program may use at most 192 MiB of HBM per device.

v0:
```python
import jax
import jax.numpy as jnp
from jax import lax
from jax.sharding import PartitionSpec as P

EXPERTS = 16
SPLIT = 2
CAP = 20


norm_eps = 1e-06


def swapped(block, axis, distance):
    count = lax.axis_size(axis)
    route = []
    for low in range(count):
        high = low | 1 << distance
        if high != low and high < count:
            route += [(low, high), (high, low)]
    return lax.ppermute(block, axis, route)


def modulate(tokens, shift, scale):
    values = tokens.astype(jnp.float32)
    center = jnp.mean(values, axis=-1, keepdims=True)
    spread = jnp.mean(jnp.square(values - center), axis=-1, keepdims=True)
    normal = (values - center) * lax.rsqrt(spread + norm_eps)
    return (normal * (1.0 + scale) + shift).astype(jnp.bfloat16)


def slot_index(block_ids):
    flat_ids = block_ids.reshape(-1)
    one_hot = (flat_ids[:, None] == jnp.arange(EXPERTS, dtype=jnp.int32)[None, :]).astype(jnp.int32)
    earlier = jnp.cumsum(one_hot, axis=0, dtype=jnp.int32) - one_hot
    slots = jnp.sum(earlier * one_hot, axis=1, dtype=jnp.int32)
    return (flat_ids * CAP + slots).reshape(block_ids.shape)


def dispatch_rows(normed, flat_index):
    targets = jnp.arange(EXPERTS * CAP, dtype=jnp.int32)
    select = jnp.sum(
        (flat_index[None, :, :] == targets[:, None, None]).astype(jnp.int32),
        axis=2,
        dtype=jnp.int32,
    )
    return jnp.dot(select.astype(jnp.bfloat16), normed, preferred_element_type=jnp.float32).astype(
        jnp.bfloat16
    )


def combine(tokens, normed, gate_row, router_weight, block_ids, flat_index, expert_out):
    logits = jnp.dot(normed, router_weight, preferred_element_type=jnp.float32)
    picked = jnp.take_along_axis(logits, block_ids, axis=1)
    gap = picked[:, 0:1] - picked[:, 1:2]
    first = jnp.take(expert_out, flat_index[:, 0], axis=0).astype(jnp.float32)
    second = jnp.take(expert_out, flat_index[:, 1], axis=0).astype(jnp.float32)
    branch = jax.nn.sigmoid(gap) * first + jax.nn.sigmoid(-gap) * second
    return (tokens.astype(jnp.float32) + gate_row[None, :] * branch).astype(jnp.bfloat16)


def expert_compute(incoming, w_in, b_in, w_out):
    columns = incoming
    pre_act = jnp.einsum(
        "urd,udf->urf",
        columns,
        lax.all_gather(w_in, "fs", axis=1, tiled=True),
        preferred_element_type=jnp.float32,
    )
    hidden = jax.nn.gelu(pre_act + b_in[:, None, :], approximate=True).astype(jnp.bfloat16)
    columns = hidden
    produced = jnp.einsum(
        "urf,ufd->urd",
        columns,
        lax.all_gather(w_out, "fs", axis=1, tiled=True),
        preferred_element_type=jnp.float32,
    )
    return produced.astype(jnp.bfloat16)


def local(hidden_states, expert_ids, modulation, router_weight, w_in, b_in, w_out):
    token_count = hidden_states.shape[1]
    width = hidden_states.shape[2]
    tokens = hidden_states.reshape(token_count, width)
    block_ids = expert_ids.reshape(token_count, 2)
    settings = modulation[0]
    normed = modulate(tokens, settings[0][None, :], settings[1][None, :])
    flat_index = slot_index(block_ids)
    outgoing = dispatch_rows(normed, flat_index)
    per_expert = outgoing.reshape(EXPERTS, CAP, width)
    members = lax.axis_size("ep")
    local_units = w_in.shape[0]
    paired = local_units == 1
    half_cap = CAP // 2
    if paired:
        sending = per_expert.reshape(members, half_cap, width)
    else:
        sending = per_expert
    received = lax.all_to_all(sending, "ep", split_axis=0, concat_axis=1, tiled=True)
    if paired:
        parity = lax.axis_index("ep") % 2
        partner = swapped(received, "ep", 0)
        own_blocks = received.reshape(members, half_cap, width)
        other_blocks = partner.reshape(members, half_cap, width)
        lower = jnp.where(parity == 0, own_blocks, other_blocks)
        upper = jnp.where(parity == 0, other_blocks, own_blocks)
        incoming = jnp.stack([lower, upper], axis=1).reshape(1, members * CAP, width)
    else:
        incoming = jnp.repeat(received, SPLIT, axis=0)
    produced = expert_compute(incoming, w_in, b_in, w_out)
    if paired:
        halves = produced.reshape(members, 2, half_cap, width)
        kept_rows = jnp.where(parity == 0, halves[:, 0], halves[:, 1])
        given_rows = jnp.where(parity == 0, halves[:, 1], halves[:, 0])
        partner_out = swapped(given_rows, "ep", 0)
        reply = (kept_rows.astype(jnp.float32) + partner_out.astype(jnp.float32)).astype(
            jnp.bfloat16
        )
    else:
        local_experts = local_units // SPLIT
        summed = jnp.sum(
            produced.astype(jnp.float32).reshape(local_experts, SPLIT, members, CAP, width), axis=1
        )
        reply = (
            summed.astype(jnp.bfloat16)
            .transpose(1, 0, 2, 3)
            .reshape(members, local_experts * CAP, width)
        )
    returned = lax.all_to_all(reply, "ep", split_axis=0, concat_axis=0, tiled=True)
    expert_out = returned.reshape(EXPERTS, CAP, width)
    result = combine(
        tokens,
        normed,
        settings[2],
        router_weight,
        block_ids,
        flat_index,
        expert_out.reshape(EXPERTS * CAP, width),
    )
    return result.reshape(1, token_count, width)


def solution(mesh):
    placed = (
        P(("parts", "fs"), "ep", None),
        P(("parts", "fs"), "ep", None),
        P(("parts", "fs"), None, None),
        P(),
        P("ep", "fs", None),
        P("ep", None),
        P("ep", "fs", None),
    )
    return jax.shard_map(
        local, mesh=mesh, in_specs=placed, out_specs=P(("parts", "fs"), "ep", None), check_vma=False
    )
```

profile of v0, /device:TPU:0, one launch (start us, length us, event | category | flops | bytes accessed | tf_op | source)
XLA Modules:
  0.0 587.7 jit_solution(5534716679597151099)
XLA Ops:
  6.5 0.7 all-gather.3.cloned.1.call-update
  7.3 0.7 all-gather.5.cloned.1.call-update
  8.5 0.6 reduce-window.6
  9.6 0.6 slice_reduce_fusion.2
  10.4 0.2 fusion.12
  10.7 0.5 convolution_convert_fusion.1
  11.1 1.1 reshape.117
  12.2 6.3 %all-to-all-start = ((bf16[16,20,1152]{2,1,0:T(8,128)(2,1)}), bf16[16,20,1152]{2,1,0:T(8,128)(2,1)S(1)}, u32[]{:S(2)}, u32[]{:S(2)}) async-start(bf16[16,20,1152]{2,1,0:T(8,128)(2,1)} %reshape.117), calls=%async_computation | async-start | bytes 1769472 | tf_op jit(solution)/shard_map/all_to_all | solution.py:99
  18.6 0.9 fusion.32
  19.5 21.3 %all-to-all-done = bf16[16,20,1152]{2,1,0:T(8,128)(2,1)S(1)} async-done(((bf16[16,20,1152]{2,1,0:T(8,128)(2,1)}), bf16[16,20,1152]{2,1,0:T(8,128)(2,1)S(1)}, u32[]{:S(2)}, u32[]{:S(2)}) %all-to-all-start) | async-done | bytes 737312 | tf_op jit(solution)/shard_map/all_to_all | solution.py:99
  40.8 0.3 copy.63
  41.2 223.4 %all-gather.3.cloned.1.call-done = bf16[8,1152,2304]{2,1,0:T(8,128)(2,1)} async-done(((bf16[8,288,2304]{2,1,0:T(8,128)(2,1)}), bf16[8,1152,2304]{2,1,0:T(8,128)(2,1)}) %all-gather.3.cloned.1.call-update) | async-done | bytes 42467344 | tf_op jit(solution)/shard_map/all_gather | solution.py:67
  264.6 254.5 %all-gather.5.cloned.1.call-done = bf16[8,2304,1152]{2,1,0:T(8,128)(2,1)} async-done(((bf16[8,576,1152]{2,1,0:T(8,128)(2,1)}), bf16[8,2304,1152]{2,1,0:T(8,128)(2,1)}) %all-gather.5.cloned.1.call-update) | async-done | bytes 42467344 | tf_op jit(solution)/shard_map/all_gather | solution.py:75
  519.2 30.4 %convolution_convert_fusion = bf16[8,80,1152]{2,1,0:T(8,128)(2,1)} fusion(bf16[8,2304,1152]{2,1,0:T(8,128)(2,1)} %all-gather.5.cloned.1.call-done, bf16[8,80,1152]{2,1,0:T(8,128)(2,1)S(1)} %bitcast.85, bf16[8,1152,2304]{2,1,0:T(8,128)(2,1)} %all-gather.3.cloned.1.call-done, f32[8,2304]{1,0:T(8,128)S(1)} %copy-done.11), kind=kOutput, calls=%fused_computation.12 | convolution fusion | flops 6810255360 | bytes 87957504 | tf_op jit(solution)/shard_map/urf,ufd->urd/dot_general | solution.py:72
  549.5 2.3 reshape.151
  551.8 0.8 reduce.1
  552.7 0.3 copy.70
  553.0 0.9 copy.67
  553.9 4.6 all-to-all-start.1
  559.0 2.0 gather_fusion
  561.3 16.7 %all-to-all-done.1 = bf16[4,80,1152]{2,1,0:T(8,128)(2,1)S(1)} async-done(((bf16[4,80,1152]{2,1,0:T(8,128)(2,1)}), bf16[4,80,1152]{2,1,0:T(8,128)(2,1)S(1)}, u32[]{:S(2)}, u32[]{:S(2)}) %all-to-all-start.1) | async-done | bytes 737312 | tf_op jit(solution)/shard_map/all_to_all | solution.py:129
  578.0 0.9 gather_fusion.2
  578.9 0.9 gather_fusion.1
  579.8 1.1 fusion.17
  (55 shorter events, 2.1 us)
Async XLA Ops:
  6.5 12.0 %copy-start = (bf16[1152,16]{0,1:T(8,128)(2,1)S(1)}, bf16[1152,16]{0,1:T(8,128)(2,1)}, u32[]{:S(2)}) copy-start(bf16[1152,16]{0,1:T(8,128)(2,1)} %param.12) | copy-start | bytes 110596
  6.5 258.0 %all-gather.3.cloned.1.call-start = ((), (), s32[]{:S(2)}) async-start(), calls=%async_computation.2 | async-start | bytes 53084160 | tf_op jit(solution)/shard_map/all_gather | solution.py:67
  7.3 0.8 copy-start.6
  7.3 2.3 copy-start.8
  7.3 3.0 copy-start.3
  7.3 511.8 %all-gather.5.cloned.1.call-start = ((), (), s32[]{:S(2)}) async-start(), calls=%async_computation.3 | async-start | bytes 53084160 | tf_op jit(solution)/shard_map/all_gather | solution.py:75
  8.4 510.7 %copy-start.11 = (f32[8,2304]{1,0:T(8,128)S(1)}, f32[8,2304]{1,0:T(8,128)}, u32[]{:S(2)}) copy-start(f32[8,2304]{1,0:T(8,128)} %param.14) | copy-start | bytes 221188
  9.4 1.3 copy-start.9
  12.2 28.6 %all-to-all-start = ((bf16[16,20,1152]{2,1,0:T(8,128)(2,1)}), bf16[16,20,1152]{2,1,0:T(8,128)(2,1)S(1)}, u32[]{:S(2)}, u32[]{:S(2)}) async-start(bf16[16,20,1152]{2,1,0:T(8,128)(2,1)} %reshape.117), calls=%async_computation | async-start | bytes 1769472 | tf_op jit(solution)/shard_map/all_to_all | solution.py:99
  549.5 9.0 %copy-start.7 = (s32[1,128,2]{1,2,0:T(2,128)S(1)}, s32[1,128,2]{1,2,0:T(2,128)}, u32[]{:S(2)}) copy-start(s32[1,128,2]{1,2,0:T(2,128)} %param.10) | copy-start | bytes 3076
  549.5 9.0 %copy-start.10 = (s32[256]{0:T(256)S(1)}, s32[256]{0:T(256)}, u32[]{:S(2)}) copy-start(s32[256]{0:T(256)} %copy-done.9) | copy-start | bytes 3076
  549.5 9.4 %copy-start.2 = (f32[128,16]{0,1:T(8,128)S(1)}, f32[128,16]{0,1:T(8,128)}, u32[]{:S(2)}) copy-start(f32[128,16]{0,1:T(8,128)} %fusion.32) | copy-start | bytes 24580
  553.9 24.1 %all-to-all-start.1 = ((bf16[4,80,1152]{2,1,0:T(8,128)(2,1)}), bf16[4,80,1152]{2,1,0:T(8,128)(2,1)S(1)}, u32[]{:S(2)}, u32[]{:S(2)}) async-start(bf16[4,80,1152]{2,1,0:T(8,128)(2,1)} %copy.67), calls=%async_computation.1 | async-start | bytes 1474560 | tf_op jit(solution)/shard_map/all_to_all | solution.py:129
  558.9 20.8 %copy-start.4 = (bf16[1,128,1152]{2,1,0:T(8,128)(2,1)S(1)}, bf16[1,128,1152]{2,1,0:T(8,128)(2,1)}, u32[]{:S(2)}) copy-start(bf16[1,128,1152]{2,1,0:T(8,128)(2,1)} %param.9) | copy-start | bytes 884740
  558.9 20.8 %copy-start.5 = (f32[1152]{0:T(1024)S(1)}, f32[1152]{0:T(1024)}, u32[]{:S(2)}) copy-start(f32[1152]{0:T(1024)} %get-tuple-element.6) | copy-start | bytes 13828
  559.0 21.9 %copy-start.1 = (bf16[1152,16]{0,1:T(8,128)(2,1)S(1)}, bf16[1152,16]{0,1:T(8,128)(2,1)}, u32[]{:S(2)}) copy-start(bf16[1152,16]{0,1:T(8,128)(2,1)} %param.12) | copy-start | bytes 110596
Sparse Core Ops, SparseCore 0:
  8.9 255.5 all-gather.2
  266.1 252.8 all-gather.4
where the time goes:
time: 588 us
  waiting for transfers between devices  517 us (88%)
  matrix products  31.7 us (5%)
  between operations  13.7 us (2%)
  starting transfers between devices  11 us (2%)
  local copies, waits for them, and re-layouts  10.3 us (2%)
    all_gather x1, waiting for transfers between devices, expert_compute(): lax.all_gather(w_out, 'fs', axis=1, tiled=True)  254 us
    all_gather x1, waiting for transfers between devices, expert_compute(): lax.all_gather(w_in, 'fs', axis=1, tiled=True)  223 us
    dot_general x1, matrix products, expert_compute(): jnp.einsum('urf,ufd->urd', columns, lax.all_gather(w_out, 'fs', axis=1, t...  30.4 us
    all_to_all x1, waiting for transfers between devices, local(): lax.all_to_all(sending, 'ep', split_axis=0, concat_axis=1, tiled=True)  21.3 us
    all_to_all x1, waiting for transfers between devices, local(): lax.all_to_all(reply, 'ep', split_axis=0, concat_axis=0, tiled=True)  16.7 us
  transfers between devices with their start and end apart: 4, of which 4 were waited for; matrix products, arithmetic and copies ran while one was open for 1% of the time, Pallas kernels for 0%

commit v1 on v0

--- a/solution.py
+++ b/solution.py
@@ -140,7 +140,125 @@
     return result.reshape(1, token_count, width)
 
 
+def fetched(block, axes, bit):
+    count = lax.axis_size(axes)
+    return lax.ppermute(block, axes, [(i, i ^ bit) for i in range(count)])
+
+
+def one_hot(index, count):
+    return (index[:, None] == jnp.arange(count, dtype=jnp.int32)[None, :]).astype(jnp.bfloat16)
+
+
+def flat_slots(block_ids):
+    flat_ids = block_ids.reshape(-1)
+    pairs = flat_ids.shape[0]
+    hot = one_hot(flat_ids, EXPERTS)
+    order = jnp.arange(pairs, dtype=jnp.int32)
+    before = (order[None, :] < order[:, None]).astype(jnp.bfloat16)
+    earlier = jnp.dot(before, hot, preferred_element_type=jnp.float32)
+    slots = jnp.sum(earlier * hot.astype(jnp.float32), axis=1).astype(jnp.int32)
+    return (flat_ids * CAP + slots).reshape(block_ids.shape)
+
+
+def mixed(tokens, normed, gate_row, router_weight, block_ids, picks, expert_out):
+    logits = jnp.dot(normed, router_weight, preferred_element_type=jnp.float32)
+    chosen = [
+        jnp.sum(
+            jnp.where(block_ids[:, k : k + 1] == jnp.arange(EXPERTS)[None, :], logits, 0.0),
+            axis=1,
+            keepdims=True,
+        )
+        for k in range(2)
+    ]
+    gap = chosen[0] - chosen[1]
+    first = jnp.dot(picks[0], expert_out, preferred_element_type=jnp.float32)
+    second = jnp.dot(picks[1], expert_out, preferred_element_type=jnp.float32)
+    branch = jax.nn.sigmoid(gap) * first + jax.nn.sigmoid(-gap) * second
+    return (tokens.astype(jnp.float32) + gate_row[None, :] * branch).astype(jnp.bfloat16)
+
+
+def local_spread(hidden_states, expert_ids, modulation, router_weight, w_in, b_in, w_out):
+    token_count = hidden_states.shape[1]
+    width = hidden_states.shape[2]
+    parts, members, shards = (lax.axis_size(a) for a in ("parts", "ep", "fs"))
+    part, shard = lax.axis_index("parts"), lax.axis_index("fs")
+    units = w_in.shape[0] // parts
+    experts = units // SPLIT
+    depth = w_in.shape[1]
+    cols = w_in.shape[2] // shards
+
+    mine = lax.dynamic_slice_in_dim(w_in, part * units, units, 0)
+    strips = []
+    for bit in range(shards):
+        strip = lax.dynamic_slice_in_dim(mine, (shard ^ bit) * cols, cols, 2)
+        strips.append(strip if bit == 0 else fetched(strip, "fs", bit))
+    bias = lax.dynamic_slice(b_in, (part * units, shard * cols), (units, cols))
+    second_w = lax.dynamic_slice_in_dim(w_out, part * units, units, 0)
+
+    tokens = hidden_states.reshape(token_count, width)
+    block_ids = expert_ids.reshape(token_count, 2)
+    settings = modulation[0]
+    normed = modulate(tokens, settings[0][None, :], settings[1][None, :])
+    flat_index = flat_slots(block_ids)
+    picks = [one_hot(flat_index[:, k], EXPERTS * CAP) for k in range(2)]
+    outgoing = lax.dot_general(
+        picks[0] + picks[1], normed, (((0,), (0,)), ((), ())), preferred_element_type=jnp.float32
+    ).astype(jnp.bfloat16)
+    sending = outgoing.reshape(members, parts, experts * CAP, width).transpose(1, 0, 2, 3)
+    received = lax.all_to_all(
+        sending.reshape(parts * members, experts * CAP, width),
+        ("parts", "ep"),
+        split_axis=0,
+        concat_axis=0,
+        tiled=True,
+    )
+    rows = parts * members * CAP
+    own = (
+        received.reshape(parts * members, experts, CAP, width)
+        .transpose(1, 0, 2, 3)
+        .reshape(experts, rows, width)
+    )
+    across = fetched(own, "fs", 2)
+    beside = fetched(jnp.stack([own, across]), "fs", 1)
+    images = [own, beside[0], across, beside[1]]
+    incoming = jnp.concatenate(images, axis=1)
+
+    incoming = jnp.repeat(incoming, SPLIT, axis=0)
+    pre_act = bias[:, None, :]
+    for bit in range(shards):
+        piece = lax.dynamic_slice_in_dim(incoming, (shard ^ bit) * depth, depth, 2)
+        pre_act = pre_act + jnp.einsum(
+            "urd,udf->urf", piece, strips[bit], preferred_element_type=jnp.float32
+        )
+    hidden = jax.nn.gelu(pre_act, approximate=True).astype(jnp.bfloat16)
+    produced = jnp.einsum("urf,ufd->urd", hidden, second_w, preferred_element_type=jnp.float32)
+    total = jnp.sum(produced.reshape(experts, SPLIT, shards, rows, width), axis=1)
+    given = fetched(total[:, 1::2].astype(jnp.bfloat16), "fs", 1)
+    chip_sum = total[:, 0::2] + given.astype(jnp.float32)
+    far = fetched(chip_sum[:, 1].astype(jnp.bfloat16), "fs", 2)
+    summed = (chip_sum[:, 0] + far.astype(jnp.float32)).astype(jnp.bfloat16)
+    reply = summed.reshape(experts, parts * members, CAP, width).transpose(1, 0, 2, 3)
+    returned = lax.all_to_all(
+        reply.reshape(parts * members, experts * CAP, width),
+        ("parts", "ep"),
+        split_axis=0,
+        concat_axis=0,
+        tiled=True,
+    )
+    expert_out = (
+        returned.reshape(parts, members, experts * CAP, width)
+        .transpose(1, 0, 2, 3)
+        .reshape(EXPERTS * CAP, width)
+    )
+    result = mixed(
+        tokens, normed, settings[2], router_weight, block_ids, picks, expert_out
+    )
+    return result.reshape(1, token_count, width)
+
+
 def solution(mesh):
+    sizes = mesh.shape
+    spread = sizes["fs"] == 4 and EXPERTS % (sizes["ep"] * sizes["parts"]) == 0
     placed = (
         P(("parts", "fs"), "ep", None),
         P(("parts", "fs"), "ep", None),
@@ -151,5 +269,5 @@
         P("ep", "fs", None),
     )
     return jax.shard_map(
-        local, mesh=mesh, in_specs=placed, out_specs=P(("parts", "fs"), "ep", None), check_vma=False
-    )
+        local_spread if spread else local, mesh=mesh, in_specs=placed, out_specs=P(("parts", "fs"), "ep", None), check_vma=False
+    )

time: 588 us -> 215 us (0.37)
  waiting for transfers between devices: 517 us -> 85.8 us
  other arithmetic: 3.77 us -> 31.3 us
  blocking collectives: 0 us -> 27.1 us
  between operations: 13.7 us -> 0.27 us
  local copies, waits for them, and re-layouts: 10.3 us -> 22.3 us
  matrix products: 31.7 us -> 38.7 us
    all_gather x2 -> x0, waiting for transfers between devices: 478 us -> none  [the longest x1 254 us: expert_compute(): lax.all_gather(w_out, 'fs', axis=1, tiled=True)]
    ppermute x0 -> x7, waiting for transfers between devices: none -> 66.7 us  [fetched(): return lax.ppermute(block, axes, [(i, i ^ bit) for i in range(count)])]
    all_to_all x0 -> x1, blocking collectives: none -> 27.1 us  [local_spread(): lax.all_to_all(sending.reshape(parts * members, experts * CAP, width), ('...]
    all_to_all x2 -> x1, waiting for transfers between devices: 38 us -> 19.1 us  [local_spread(): lax.all_to_all(reply.reshape(parts * members, experts * CAP, width), ('pa...]
    concatenate x0 -> x1, other arithmetic: none -> 14 us  [local_spread(): incoming = jnp.concatenate(images, axis=1)]
    dynamic_slice x0 -> x2, local copies, waits for them, and re-layouts: none -> 7.87 us  [the longest x1 7.05 us: local_spread(): strip = lax.dynamic_slice_in_dim(mine, (shard ^ bit) * cols, cols, 2)]
    reduce_sum x3 -> x1, other arithmetic: 0.96 us -> 8.36 us  [local_spread(): jnp.sum(produced.reshape(experts, SPLIT, shards, rows, width), axis=1)]
    all_to_all x2 -> x1, starting transfers between devices: 10.9 us -> 3.54 us  [local_spread(): lax.all_to_all(reply.reshape(parts * members, experts * CAP, width), ('pa...]
  transfers between devices with their start and end apart: 4 -> 8, of which waited for: 4 -> 5; matrix products, arithmetic and copies ran while one was open for 1% -> 25% of each run, Pallas kernels for 0% -> 0%
where the time goes in v1:
time: 215 us; the launch traced here: 214 us
  waiting for transfers between devices  85.8 us (40%)
  matrix products  38.7 us (18%)
  other arithmetic  31.3 us (15%)
  blocking collectives  27.1 us (13%)
  local copies, waits for them, and re-layouts  22.3 us (10%)
  starting transfers between devices  8.94 us (4%)
    ppermute x7, waiting for transfers between devices, fetched(): return lax.ppermute(block, axes, [(i, i ^ bit) for i in range(count)])  66.7 us
    all_to_all x1, blocking collectives, local_spread(): lax.all_to_all(sending.reshape(parts * members, experts * CAP, width), ('...  27.1 us
    dot_general x3, matrix products, local_spread(): jnp.einsum('urd,udf->urf', piece, strips[bit], preferred_element_type=jnp...  19.7 us
    all_to_all x1, waiting for transfers between devices, local_spread(): lax.all_to_all(reply.reshape(parts * members, experts * CAP, width), ('pa...  19.1 us
    dot_general x1, matrix products, local_spread(): jnp.einsum('urf,ufd->urd', hidden, second_w, preferred_element_type=jnp.f...  15.5 us
    concatenate x1, other arithmetic, local_spread(): incoming = jnp.concatenate(images, axis=1)  14 us
    reduce_sum x1, other arithmetic, local_spread(): jnp.sum(produced.reshape(experts, SPLIT, shards, rows, width), axis=1)  8.36 us
    concatenate x1, local copies, waits for them, and re-layouts, local_spread(): incoming = jnp.concatenate(images, axis=1)  7.18 us
  transfers between devices with their start and end apart: 8, of which 5 were waited for; matrix products, arithmetic and copies ran while one was open for 25% of the time, Pallas kernels for 0%

profile of v1, /device:TPU:0, one launch (start us, length us, event | category | flops | bytes accessed | tf_op | source)
XLA Modules:
  0.0 214.3 jit_solution(1892068950975984505)
XLA Ops:
  1.1 1.2 fusion.39
  4.6 1.4 convolution_convert_fusion
  6.1 27.1 %all_to_all.10 = bf16[8,40,1152]{2,1,0:T(8,128)(2,1)S(1)} all-to-all(bf16[8,40,1152]{2,1,0:T(8,128)(2,1)S(1)} %bitcast.78), channel_id=1, replica_groups=mesh['parts'=2,'ep'=4,'fs'=4] {'parts','ep'}, dimensions={0} | all-to-all | bytes 1474560 | tf_op jit(solution)/shard_map/all_to_all | solution.py:208
  33.8 1.6 collective-permute-start
  35.4 15.6 %collective-permute-done = bf16[2,160,1152]{2,0,1:T(2,128)(2,1)S(1)} collective-permute-done((bf16[2,160,1152]{2,0,1:T(2,128)(2,1)S(1)}, bf16[2,160,1152]{2,0,1:T(2,128)(2,1)S(1)}, u32[]{:S(2)}, u32[]{:S(2)}) %collective-permute-start) | collective-permute-done | bytes 737312 | tf_op jit(solution)/shard_map/ppermute | solution.py:145
  51.0 2.1 pad_maximum_fusion.1
  53.2 7.1 %constant_dynamic-slice_fusion = (bf16[4,288,576]{2,1,0:T(8,128)(2,1)}, bf16[4,288,576]{2,1,0:T(8,128)(2,1)}, bf16[4,288,576]{2,1,0:T(8,128)(2,1)}) fusion(bf16[8,288,2304]{2,1,0:T(8,128)(2,1)} %param.11, s32[]{:T(128)S(6)} %select_n.52, s32[]{:T(128)S(6)} %select_n.62, s32[]{:T(128)S(6)} %select_n.56, s32[]{:T(128)S(6)} %select_n.59), kind=kLoop, calls=%fused_computation.80 | loop fusion | bytes 7962640 | tf_op jit(solution)/shard_map/dynamic_slice | solution.py:193
  60.2 1.6 collective-permute-start.4
  64.2 14.0 %pad_maximum_fusion = bf16[2,640,1152]{2,0,1:T(2,128)(2,1)S(1)} fusion(bf16[2,160,1152]{2,0,1:T(2,128)(2,1)S(1)} %get-tuple-element.18, bf16[2,160,1152]{2,0,1:T(2,128)(2,1)} %copy-done.4, bf16[2,160,1152]{2,0,1:T(2,128)(2,1)S(1)} %get-tuple-element.17, bf16[2,160,1152]{2,0,1:T(2,128)(2,1)} %bitcast.75), kind=kLoop, calls=%fused_computation.11 | loop fusion | flops 4423680 | bytes 5898240 | tf_op jit(solution)/shard_map/concatenate | solution.py:224
  78.2 7.2 %copy.44 = bf16[2,640,1152]{1,2,0:T(8,128)(2,1)} copy(bf16[2,640,1152]{2,0,1:T(2,128)(2,1)S(1)} %pad_maximum_fusion) | data formatting | bytes 5898240 | tf_op jit(solution)/shard_map/concatenate | solution.py:224
  85.4 2.3 %broadcast_in_dim.7 = bf16[2,2,640,1152]{2,3,1,0:T(8,128)(2,1)S(1)} broadcast(bf16[2,640,1152]{1,2,0:T(8,128)(2,1)} %copy.44), dimensions={0,2,3} | broadcast | bytes 8847360 | tf_op jit(solution)/shard_map/broadcast_in_dim | solution.py:226
  87.7 8.2 %fusion.31 = f32[4,640,576]{1,2,0:T(8,128)} fusion(bf16[8,288,2304]{2,1,0:T(8,128)(2,1)} %param.11, s32[]{:T(128)S(6)} %select_n.52, s32[]{:T(128)S(6)} %select_n.53, bf16[4,640,1152]{1,2,0:T(8,128)(2,1)S(1)} %bitcast.66, s32[]{:T(128)S(6)} %select_n.51), kind=kOutput, calls=%fused_computation.37 | convolution fusion | flops 849346560 | bytes 8847372 | tf_op jit(solution)/shard_map/urd,udf->urf/dot_general | solution.py:230
  95.9 30.8 %collective-permute-done.3 = bf16[4,288,576]{2,1,0:T(8,128)(2,1)} collective-permute-done((bf16[4,288,576]{2,1,0:T(8,128)(2,1)}, bf16[4,288,576]{2,1,0:T(8,128)(2,1)}, u32[]{:S(2)}, u32[]{:S(2)}) %collective-permute-start.3) | collective-permute-done | bytes 1327136 | tf_op jit(solution)/shard_map/ppermute | solution.py:145
  126.7 5.8 %fusion.27 = f32[4,640,576]{1,2,0:T(8,128)} fusion(bf16[4,288,576]{2,1,0:T(8,128)(2,1)} %collective-permute-done.3, bf16[4,640,1152]{1,2,0:T(8,128)(2,1)S(1)} %bitcast.67, s32[]{:T(128)S(6)} %select_n.57), kind=kOutput, calls=%fused_computation.33 | convolution fusion | flops 849346560 | bytes 8699908 | tf_op jit(solution)/shard_map/urd,udf->urf/dot_general | solution.py:230
  132.5 5.8 %fusion.29 = f32[4,640,576]{1,2,0:T(8,128)} fusion(bf16[4,288,576]{2,1,0:T(8,128)(2,1)} %collective-permute-done.2, bf16[4,640,1152]{1,2,0:T(8,128)(2,1)S(1)} %bitcast.68, s32[]{:T(128)S(6)} %select_n.54), kind=kOutput, calls=%fused_computation.35 | convolution fusion | flops 849346560 | bytes 8699908 | tf_op jit(solution)/shard_map/urd,udf->urf/dot_general | solution.py:230
  138.3 15.5 %fusion.8 = f32[4,640,1152]{2,1,0:T(8,128)} fusion(bf16[8,576,1152]{2,1,0:T(8,128)(2,1)} %param.13, s32[]{:T(128)S(6)} %select_n.49, f32[4,640,576]{1,2,0:T(8,128)} %fusion.27, f32[4,640,576]{1,2,0:T(8,128)} %fusion.29, f32[4,640,576]{1,2,0:T(8,128)} %fusion.31, f32[4,576]{1,0:T(4,128)S(1)} %dynamic_slice.35, ...), kind=kOutput, calls=%fused_computation.9 | convolution fusion | flops 4265902080 | bytes 37757960 | tf_op jit(solution)/shard_map/urf,ufd->urd/dot_general | solution.py:234
  153.8 8.4 %reduce_sum.59 = f32[2,4,160,1152]{3,2,1,0:T(8,128)} reduce(f32[2,2,4,160,1152]{4,3,2,1,0:T(8,128)} %bitcast.70, f32[]{:T(128)} %constant.90.clone.1), dimensions={1}, to_apply=%region_5.6 | reduce | flops 1474560 | bytes 17694724 | tf_op jit(solution)/shard_map/reduce_sum | solution.py:235
  162.2 3.1 %convert.6 = bf16[2,4,160,1152]{3,2,1,0:T(8,128)(2,1)S(1)} convert(f32[2,4,160,1152]{3,2,1,0:T(8,128)} %reduce_sum.59) | non-fusion elementwise | flops 1474560 | bytes 8847360 | tf_op jit(solution)/shard_map/convert.1
  165.5 3.3 %collective-permute-done.5 = bf16[2,2,160,1152]{3,2,1,0:T(8,128)(2,1)S(1)} collective-permute-done((bf16[2,2,160,1152]{3,2,1,0:T(8,128)(2,1)S(1)}, bf16[2,2,160,1152]{3,2,1,0:T(8,128)(2,1)S(1)}, u32[]{:S(2)}, u32[]{:S(2)}) %collective-permute-start.5) | collective-permute-done | bytes 1474592 | tf_op jit(solution)/shard_map/ppermute | solution.py:145
  169.2 1.6 collective-permute-start.6
  170.8 17.0 %collective-permute-done.6 = bf16[2,160,1152]{2,1,0:T(8,128)(2,1)S(1)} collective-permute-done((bf16[2,160,1152]{2,1,0:T(8,128)(2,1)S(1)}, bf16[2,160,1152]{2,1,0:T(8,128)(2,1)S(1)}, u32[]{:S(2)}, u32[]{:S(2)}) %collective-permute-start.6) | collective-permute-done | bytes 737312 | tf_op jit(solution)/shard_map/ppermute | solution.py:145
  189.6 3.5 %all-to-all-start.1 = ((bf16[8,40,1152]{2,1,0:T(8,128)(2,1)}), bf16[8,40,1152]{2,1,0:T(8,128)(2,1)S(1)}, u32[]{:S(2)}, u32[]{:S(2)}) async-start(bf16[8,40,1152]{2,1,0:T(8,128)(2,1)} %copy.48), calls=%async_computation.1 | async-start | bytes 1474560 | tf_op jit(solution)/shard_map/all_to_all | solution.py:241
  193.7 19.1 %all-to-all-done.1 = bf16[8,40,1152]{2,1,0:T(8,128)(2,1)S(1)} async-done(((bf16[8,40,1152]{2,1,0:T(8,128)(2,1)}), bf16[8,40,1152]{2,1,0:T(8,128)(2,1)S(1)}, u32[]{:S(2)}, u32[]{:S(2)}) %all-to-all-start.1) | async-done | bytes 737312 | tf_op jit(solution)/shard_map/all_to_all | solution.py:241
  213.2 1.1 fusion.22
  (47 shorter events, 9.8 us)
Async XLA Ops:
  0.0 193.4 %copy-start = (bf16[1152,16]{0,1:T(8,128)(2,1)S(1)}, bf16[1152,16]{0,1:T(8,128)(2,1)}, u32[]{:S(2)}) copy-start(bf16[1152,16]{0,1:T(8,128)(2,1)} %param.10) | copy-start | bytes 110596
  33.8 17.2 %copy-start.3 = (bf16[2,8,20,1152]{3,0,2,1:T(2,128)(2,1)}, bf16[2,8,20,1152]{3,0,2,1:T(2,128)(2,1)S(1)}, u32[]{:S(2)}) copy-start(bf16[2,8,20,1152]{3,0,2,1:T(2,128)(2,1)S(1)} %copy.42) | copy-start | bytes 2211844
  33.8 17.2 %collective-permute-start = (bf16[2,160,1152]{2,0,1:T(2,128)(2,1)S(1)}, bf16[2,160,1152]{2,0,1:T(2,128)(2,1)S(1)}, u32[]{:S(2)}, u32[]{:S(2)}) collective-permute-start(bf16[2,160,1152]{2,0,1:T(2,128)(2,1)S(1)} %bitcast.73), channel_id=1, source_target_pairs={{0,2},{1,3},{2,0},{3,1},{4,6},{5,7},{6,4},{7,5},{8,10},{9,11},{10,... | collective-permute-start | bytes 2211848 | tf_op jit(solution)/shard_map/ppermute | solution.py:145
  51.0 2.1 copy-start.4
  53.1 10.1 %collective-permute-start.1 = (bf16[2,2,160,1152]{3,1,2,0:T(2,128)(2,1)S(1)}, bf16[2,2,160,1152]{3,1,2,0:T(2,128)(2,1)S(1)}, u32[]{:S(2)}, u32[]{:S(2)}) collective-permute-start(bf16[2,2,160,1152]{3,1,2,0:T(2,128)(2,1)S(1)} %pad_maximum_fusion.1), channel_id=1, source_target_pairs={{0,1},{1,0},{2,3},{3,2},{4,5},{5,4},{6,7},{7,6},{8,9},{9,8},{10,11... | collective-permute-start | bytes 4423688 | tf_op jit(solution)/shard_map/ppermute | solution.py:145
  60.2 78.0 %collective-permute-start.4 = (bf16[4,288,576]{2,1,0:T(8,128)(2,1)}, bf16[4,288,576]{2,1,0:T(8,128)(2,1)}, u32[]{:S(2)}, u32[]{:S(2)}) collective-permute-start(bf16[4,288,576]{2,1,0:T(8,128)(2,1)} %get-tuple-element.14), channel_id=1, source_target_pairs={{0,3},{1,2},{2,1},{3,0},{4,7},{5,6},{6,5},{7,4},{8,11},{9,10},{10,... | collective-permute-start | bytes 3981320 | tf_op jit(solution)/shard_map/ppermute | solution.py:145
  61.9 70.6 %collective-permute-start.2 = (bf16[4,288,576]{2,1,0:T(8,128)(2,1)}, bf16[4,288,576]{2,1,0:T(8,128)(2,1)}, u32[]{:S(2)}, u32[]{:S(2)}) collective-permute-start(bf16[4,288,576]{2,1,0:T(8,128)(2,1)} %get-tuple-element.15), channel_id=1, source_target_pairs={{0,1},{1,0},{2,3},{3,2},{4,5},{5,4},{6,7},{7,6},{8,9},{9,8},{10,11... | collective-permute-start | bytes 3981320 | tf_op jit(solution)/shard_map/ppermute | solution.py:145
  61.9 64.9 %collective-permute-start.3 = (bf16[4,288,576]{2,1,0:T(8,128)(2,1)}, bf16[4,288,576]{2,1,0:T(8,128)(2,1)}, u32[]{:S(2)}, u32[]{:S(2)}) collective-permute-start(bf16[4,288,576]{2,1,0:T(8,128)(2,1)} %get-tuple-element.16), channel_id=1, source_target_pairs={{0,2},{1,3},{2,0},{3,1},{4,6},{5,7},{6,4},{7,5},{8,10},{9,11},{10,... | collective-permute-start | bytes 3981320 | tf_op jit(solution)/shard_map/ppermute | solution.py:145
  87.7 44.8 %copy-start.2 = (bf16[2,2,640,1152]{2,3,1,0:T(8,128)(2,1)}, bf16[2,2,640,1152]{2,3,1,0:T(8,128)(2,1)S(1)}, u32[]{:S(2)}) copy-start(bf16[2,2,640,1152]{2,3,1,0:T(8,128)(2,1)S(1)} %broadcast_in_dim.7) | copy-start | bytes 17694724
  162.2 6.6 %copy-start.1 = (f32[2,4,160,1152]{3,2,1,0:T(8,128)S(1)}, f32[2,4,160,1152]{3,2,1,0:T(8,128)}, u32[]{:S(2)}) copy-start(f32[2,4,160,1152]{3,2,1,0:T(8,128)} %reduce_sum.59) | copy-start | bytes 17694724
  165.4 3.3 %collective-permute-start.5 = (bf16[2,2,160,1152]{3,2,1,0:T(8,128)(2,1)S(1)}, bf16[2,2,160,1152]{3,2,1,0:T(8,128)(2,1)S(1)}, u32[]{:S(2)}, u32[]{:S(2)}) collective-permute-start(bf16[2,2,160,1152]{3,2,1,0:T(8,128)(2,1)S(1)} %slice.54), channel_id=1, source_target_pairs={{0,1},{1,0},{2,3},{3,2},{4,5},{5,4},{6,7},{7,6},{8,9},{9,8},{10,11... | collective-permute-start | bytes 4423688 | tf_op jit(solution)/shard_map/ppermute | solution.py:145
  169.2 18.6 %collective-permute-start.6 = (bf16[2,160,1152]{2,1,0:T(8,128)(2,1)S(1)}, bf16[2,160,1152]{2,1,0:T(8,128)(2,1)S(1)}, u32[]{:S(2)}, u32[]{:S(2)}) collective-permute-start(bf16[2,160,1152]{2,1,0:T(8,128)(2,1)S(1)} %fusion.35), channel_id=1, source_target_pairs={{0,2},{1,3},{2,0},{3,1},{4,6},{5,7},{6,4},{7,5},{8,10},{9,11},{10,... | collective-permute-start | bytes 2211848 | tf_op jit(solution)/shard_map/ppermute | solution.py:145
  188.0 5.4 %copy-start.5 = (bf16[1,128,1152]{2,1,0:T(8,128)(2,1)S(1)}, bf16[1,128,1152]{2,1,0:T(8,128)(2,1)}, u32[]{:S(2)}) copy-start(bf16[1,128,1152]{2,1,0:T(8,128)(2,1)} %param.7) | copy-start | bytes 884740
  189.6 23.2 %all-to-all-start.1 = ((bf16[8,40,1152]{2,1,0:T(8,128)(2,1)}), bf16[8,40,1152]{2,1,0:T(8,128)(2,1)S(1)}, u32[]{:S(2)}, u32[]{:S(2)}) async-start(bf16[8,40,1152]{2,1,0:T(8,128)(2,1)} %copy.48), calls=%async_computation.1 | async-start | bytes 1474560 | tf_op jit(solution)/shard_map/all_to_all | solution.py:241

commit v2 on v0

--- a/solution.py
+++ b/solution.py
@@ -1,6 +1,10 @@
+import functools
+
 import jax
 import jax.numpy as jnp
 from jax import lax
+from jax.experimental import pallas as pl
+from jax.experimental.pallas import tpu as pltpu
 from jax.sharding import PartitionSpec as P
 
 EXPERTS = 16
@@ -140,7 +144,312 @@
     return result.reshape(1, token_count, width)
 
 
+def one_hot(index, count):
+    return (index[:, None] == jnp.arange(count, dtype=jnp.int32)[None, :]).astype(jnp.bfloat16)
+
+
+def flat_slots(block_ids):
+    flat_ids = block_ids.reshape(-1)
+    pairs = flat_ids.shape[0]
+    hot = one_hot(flat_ids, EXPERTS)
+    order = jnp.arange(pairs, dtype=jnp.int32)
+    before = (order[None, :] < order[:, None]).astype(jnp.bfloat16)
+    earlier = jnp.dot(before, hot, preferred_element_type=jnp.float32)
+    slots = jnp.sum(earlier * hot.astype(jnp.float32), axis=1).astype(jnp.int32)
+    return (flat_ids * CAP + slots).reshape(block_ids.shape)
+
+
+def mixed(tokens, normed, gate_row, router_weight, block_ids, picks, expert_out):
+    logits = jnp.dot(normed, router_weight, preferred_element_type=jnp.float32)
+    chosen = [
+        jnp.sum(
+            jnp.where(block_ids[:, k : k + 1] == jnp.arange(EXPERTS)[None, :], logits, 0.0),
+            axis=1,
+            keepdims=True,
+        )
+        for k in range(2)
+    ]
+    gap = chosen[0] - chosen[1]
+    first = jnp.dot(picks[0], expert_out, preferred_element_type=jnp.float32)
+    second = jnp.dot(picks[1], expert_out, preferred_element_type=jnp.float32)
+    branch = jax.nn.sigmoid(gap) * first + jax.nn.sigmoid(-gap) * second
+    return (tokens.astype(jnp.float32) + gate_row[None, :] * branch).astype(jnp.bfloat16)
+
+
+LANES = 128
+PADDED = 64
+
+
+def flip(index, bit):
+    return index + bit * (1 - 2 * ((index // bit) % 2))
+
+
+def flipped(index, distance, count):
+    bit = 1
+    while bit < count:
+        if distance & bit:
+            index = flip(index, bit)
+        bit *= 2
+    return index
+
+
+def expert_kernel(
+    sizes, send_ref, w_in_ref, bias_ref, w_out_ref, out_ref,
+    got, rows_in, first_w, second_w, acc, r1_out, r1_in, r2_out, r2_in, r3_out,
+    w_send, w_recv, second_sem, t1_send, t1_recv, t2_send, t2_recv,
+    t3_send, t3_recv, t4_send, t4_recv,
+    r1_send, r1_recv, r2_send, r2_recv, r3_send, r3_recv,
+):
+    parts, members, experts, units, cols, span, depth = sizes
+    group = parts * members
+    part, member, shard = (lax.axis_index(n) for n in ("parts", "ep", "fs"))
+
+    def block_peer(d):
+        return {
+            "parts": flipped(part, d // members, parts),
+            "ep": flipped(member, d % members, members),
+            "fs": shard,
+        }
+
+    def shard_peer(bit):
+        return {"parts": part, "ep": member, "fs": flipped(shard, bit, 4)}
+
+    def remote(src, dst, send, recv, peer):
+        return pltpu.make_async_remote_copy(
+            src_ref=src, dst_ref=dst, send_sem=send, recv_sem=recv,
+            device_id=peer, device_id_type=pl.DeviceIdType.MESH,
+        )
+
+    barrier = pltpu.get_barrier_semaphore()
+    peers = [block_peer(d) for d in range(1, group)] + [shard_peer(b) for b in range(1, 4)]
+    for peer in peers:
+        pl.semaphore_signal(
+            barrier, inc=1, device_id=peer, device_id_type=pl.DeviceIdType.MESH
+        )
+    pl.semaphore_wait(barrier, len(peers))
+
+    def strip(u, bit):
+        target = flipped(shard, bit, 4)
+        start = pl.multiple_of((target * cols) // LANES * LANES, LANES)
+        src = w_in_ref.at[part * units + u, :, pl.ds(start, span)]
+        dst = first_w.at[u, pl.ds(pl.multiple_of(shard * depth, 32), depth), :]
+        if bit == 0:
+            return pltpu.make_async_copy(src, dst, w_recv.at[u, 0])
+        return remote(src, dst, w_send.at[u, bit], w_recv.at[u, bit], shard_peer(bit))
+
+    offset = (shard * cols) % LANES
+
+    def second(u):
+        place = pl.ds(pl.multiple_of(offset, PADDED), cols)
+        return pltpu.make_async_copy(
+            w_out_ref.at[part * units + u], second_w.at[u, place, :], second_sem.at[u]
+        )
+
+    def t1(d):
+        if d == 0:
+            return pltpu.make_async_copy(send_ref.at[0], got.at[0, 0], t1_recv.at[0])
+        return remote(send_ref.at[d], got.at[0, d], t1_send.at[d], t1_recv.at[d], block_peer(d))
+
+    def t2(d):
+        return remote(got.at[0, d], got.at[2, d], t2_send.at[d], t2_recv.at[d], shard_peer(2))
+
+    def t3(d):
+        return remote(got.at[0, d], got.at[1, d], t3_send.at[d], t3_recv.at[d], shard_peer(1))
+
+    def t4(d):
+        return remote(got.at[2, d], got.at[3, d], t4_send.at[d], t4_recv.at[d], shard_peer(1))
+
+    def r1(e):
+        return remote(r1_out.at[e], r1_in.at[e], r1_send.at[e], r1_recv.at[e], shard_peer(1))
+
+    def r2(e):
+        return remote(r2_out.at[e], r2_in.at[e], r2_send.at[e], r2_recv.at[e], shard_peer(2))
+
+    def r3(e, d):
+        src, dst = r3_out.at[e, d], out_ref.at[d, e]
+        if d == 0:
+            return pltpu.make_async_copy(src, dst, r3_recv.at[e, 0])
+        return remote(src, dst, r3_send.at[e, d], r3_recv.at[e, d], block_peer(d))
+
+    for d in range(group):
+        t1(d).start()
+    early = units // experts
+    for u in range(early):
+        for bit in (2, 3, 1, 0):
+            strip(u, bit).start()
+    if span > cols:
+        spare = (1 - offset // PADDED) * cols
+        for u in range(units):
+            second_w[u, pl.ds(pl.multiple_of(spare, PADDED), span - cols), :] = jnp.zeros(
+                (span - cols, second_w.shape[2]), second_w.dtype
+            )
+    for u in range(units):
+        second(u).start()
+
+    def arrived(copy, d):
+        if d == 0:
+            copy.wait()
+        else:
+            copy.wait_recv()
+
+    for d in range(group):
+        arrived(t1(d), d)
+        t2(d).start()
+        t3(d).start()
+    for u in range(early, units):
+        for bit in (2, 3, 1, 0):
+            strip(u, bit).start()
+    for d in range(group):
+        t2(d).wait_recv()
+        t4(d).start()
+
+    half = group * CAP
+    batch = 4 if group % 4 == 0 else 1
+
+    def arrange(images, side):
+        for place, image in enumerate(images):
+            for low in range(0, group, batch):
+                chunks = [got[image, low + i] for i in range(batch)]
+                for e in range(experts):
+                    rows_in[e, side, pl.ds(place * half + low * CAP, batch * CAP), :] = (
+                        jnp.concatenate([c[e * CAP : (e + 1) * CAP] for c in chunks], axis=0)
+                    )
+
+    arrange((0, 2), 0)
+    for d in range(group):
+        t3(d).wait_recv()
+        t4(d).wait_recv()
+    arrange((1, 3), 1)
+
+    def reply(e):
+        r2(e).wait_recv()
+        total = acc_keep(e) + r2_in[e].astype(jnp.float32)
+        total = total.astype(jnp.bfloat16)
+        for d in range(group):
+            r3_out[e, d] = total[d * CAP : (d + 1) * CAP]
+        for d in range(group):
+            r3(e, d).start()
+
+    def acc_keep(e):
+        return acc[e, 0, 0:half, :]
+
+    for e in range(experts):
+        for p in range(SPLIT):
+            u = e * SPLIT + p
+            strip(u, 0).wait()
+            for bit in (1, 2, 3):
+                strip(u, bit).wait_recv()
+            second(u).wait()
+            for side in (1, 0):
+                pre = jnp.dot(
+                    rows_in[e, side], first_w[u], preferred_element_type=jnp.float32
+                )
+                hidden = jax.nn.gelu(pre + bias_ref[u], approximate=True).astype(jnp.bfloat16)
+                made = jnp.dot(hidden, second_w[u], preferred_element_type=jnp.float32)
+                if p > 0:
+                    made = made + acc[e, side]
+                if p == SPLIT - 1 and side == 1:
+                    r1_out[e] = made.astype(jnp.bfloat16)
+                    r1(e).start()
+                else:
+                    acc[e, side] = made
+            if p == 0 and e > 0:
+                reply(e - 1)
+        r1(e).wait_recv()
+        chip = acc[e, 0] + r1_in[e].astype(jnp.float32)
+        r2_out[e] = chip[half:].astype(jnp.bfloat16)
+        r2(e).start()
+        acc[e, 0] = chip
+    reply(experts - 1)
+
+    for e in range(experts):
+        for d in range(group):
+            arrived(r3(e, d), d)
+            if d > 0:
+                r3(e, d).wait_send()
+        r1(e).wait_send()
+        r2(e).wait_send()
+    for u in range(units):
+        for bit in (1, 2, 3):
+            strip(u, bit).wait_send()
+    for d in range(group):
+        if d > 0:
+            t1(d).wait_send()
+        t2(d).wait_send()
+        t3(d).wait_send()
+        t4(d).wait_send()
+
+
+def local_spread(hidden_states, expert_ids, modulation, router_weight, w_in, b_in, w_out):
+    token_count = hidden_states.shape[1]
+    width = hidden_states.shape[2]
+    parts, members, shards = (lax.axis_size(a) for a in ("parts", "ep", "fs"))
+    part, member, shard = (lax.axis_index(a) for a in ("parts", "ep", "fs"))
+    group = parts * members
+    units = w_in.shape[0] // parts
+    experts = units // SPLIT
+    depth = w_in.shape[1]
+    cols = w_in.shape[2] // shards
+    span = cols + cols % LANES
+
+    start = shard * cols // LANES * LANES
+    bias = lax.dynamic_slice(b_in, (part * units, start), (units, span))[:, None, :]
+
+    tokens = hidden_states.reshape(token_count, width)
+    block_ids = expert_ids.reshape(token_count, 2)
+    settings = modulation[0]
+    normed = modulate(tokens, settings[0][None, :], settings[1][None, :])
+    slots = flat_slots(block_ids) - block_ids * CAP
+    holder_member = block_ids // (parts * experts)
+    holder_part = block_ids // experts % parts
+    distance = (holder_part * members + holder_member) ^ (part * members + member)
+    place = (distance * experts + block_ids % experts) * CAP + slots
+    picks = [one_hot(place[:, k], EXPERTS * CAP) for k in range(2)]
+    sending = lax.dot_general(
+        picks[0] + picks[1], normed, (((0,), (0,)), ((), ())), preferred_element_type=jnp.float32
+    ).astype(jnp.bfloat16)
+
+    rows = 2 * group * CAP
+    bf16, dma = jnp.bfloat16, pltpu.SemaphoreType.DMA
+    hbm, vmem = pl.BlockSpec(memory_space=pl.ANY), pl.BlockSpec(memory_space=pltpu.VMEM)
+    sizes = (parts, members, experts, units, cols, span, depth)
+    returned = pl.pallas_call(
+        functools.partial(expert_kernel, sizes),
+        out_shape=jax.ShapeDtypeStruct((group, experts, CAP, width), bf16),
+        in_specs=[hbm, hbm, vmem, hbm],
+        out_specs=hbm,
+        scratch_shapes=[
+            pltpu.VMEM((shards, group, experts * CAP, width), bf16),
+            pltpu.VMEM((experts, 2, rows, width), bf16),
+            pltpu.VMEM((units, width, span), bf16),
+            pltpu.VMEM((units, span, width), bf16),
+            pltpu.VMEM((experts, 2, rows, width), jnp.float32),
+            pltpu.VMEM((experts, rows, width), bf16),
+            pltpu.VMEM((experts, rows, width), bf16),
+            pltpu.VMEM((experts, rows // 2, width), bf16),
+            pltpu.VMEM((experts, rows // 2, width), bf16),
+            pltpu.VMEM((experts, group, CAP, width), bf16),
+            dma((units, 4)), dma((units, 4)), dma((units,)),
+        ]
+        + [dma((group,))] * 8
+        + [dma((experts,))] * 4
+        + [dma((experts, group))] * 2,
+        compiler_params=pltpu.CompilerParams(
+            collective_id=0, has_side_effects=True, vmem_limit_bytes=60 * 1024 * 1024
+        ),
+    )(sending.reshape(group, experts * CAP, width), w_in, bias, w_out)
+
+    expert_out = returned.reshape(EXPERTS * CAP, width)
+    result = mixed(
+        tokens, normed, settings[2], router_weight, block_ids, picks, expert_out
+    )
+    return result.reshape(1, token_count, width)
+
+
 def solution(mesh):
+    sizes = mesh.shape
+    group = sizes["ep"] * sizes["parts"]
+    spread = sizes["fs"] == 4 and EXPERTS % group == 0
     placed = (
         P(("parts", "fs"), "ep", None),
         P(("parts", "fs"), "ep", None),
@@ -151,5 +460,5 @@
         P("ep", "fs", None),
     )
     return jax.shard_map(
-        local, mesh=mesh, in_specs=placed, out_specs=P(("parts", "fs"), "ep", None), check_vma=False
-    )
+        local_spread if spread else local, mesh=mesh, in_specs=placed, out_specs=P(("parts", "fs"), "ep", None), check_vma=False
+    )

time: 588 us -> 135 us (0.23)
  waiting for transfers between devices: 517 us -> 0 us
  Pallas kernels: 0 us -> 121 us
  matrix products: 31.7 us -> 5.27 us
  between operations: 13.7 us -> 0.09 us
  starting transfers between devices: 11 us -> 0 us
  local copies, waits for them, and re-layouts: 10.3 us -> 4.14 us
    all_gather x2 -> x0, waiting for transfers between devices: 478 us -> none  [the longest x1 254 us: expert_compute(): lax.all_gather(w_out, 'fs', axis=1, tiled=True)]
    pallas_call x0 -> x1, Pallas kernels: none -> 121 us  [local_spread(): pl.pallas_call(functools.partial(expert_kernel, sizes), out_shape=jax.Sha...]
    all_to_all x2 -> x0, waiting for transfers between devices: 38 us -> none  [the longest x1 21.3 us: local(): lax.all_to_all(sending, 'ep', split_axis=0, concat_axis=1, tiled=True)]
    dot_general x3 -> x5, matrix products: 31.7 us -> 5.27 us  [the longest x1 2.32 us: local_spread(): lax.dot_general(picks[0] + picks[1], normed, (((0,), (0,)), ((), ())), pr...]
    all_to_all x2 -> x0, starting transfers between devices: 10.9 us -> none  [the longest x1 6.35 us: local(): lax.all_to_all(sending, 'ep', split_axis=0, concat_axis=1, tiled=True)]
  transfers between devices with their start and end apart: 4 -> 0, of which waited for: 4 -> 0; matrix products, arithmetic and copies ran while one was open for 1% -> 0% of each run, Pallas kernels for 0% -> 0%
where the time goes in v2:
time: 135 us; the launch traced here: 134 us
  Pallas kernels  121 us (90%)
  matrix products  5.27 us (4%)
  local copies, waits for them, and re-layouts  4.14 us (3%)
  other arithmetic  3.22 us (2%)
    pallas_call x1, Pallas kernels, local_spread(): pl.pallas_call(functools.partial(expert_kernel, sizes), out_shape=jax.Sha...  121 us

profile of v2, /device:TPU:0, one launch (start us, length us, event | category | flops | bytes accessed | tf_op | source)
XLA Modules:
  0.0 134.2 jit_solution(5512288052842941799)
XLA Ops:
  0.0 0.0 copy-start
  0.0 1.1 convert_reduce_fusion
  1.1 1.2 fusion.9
  2.3 0.8 dynamic_slice.3
  3.1 0.6 broadcast_in_dim.7.bias_ref
  3.7 0.8 slice_reduce_fusion.5
  4.5 0.8 copy.10
  5.3 0.1 eq.86
  5.4 0.2 fusion.5
  5.6 0.2 slice_reduce_fusion.2
  5.8 0.0 copy-done
  5.8 1.3 select_reduce_fusion
  7.1 0.1 convert_element_type.42
  7.3 0.1 fusion.29
  7.4 0.2 slice_reduce_fusion.1
  7.6 2.3 %convolution_convert_fusion = bf16[320,1152]{1,0:T(8,128)(2,1)} fusion(s32[128]{0:T(128)S(1)} %get-tuple-element.8, s32[128]{0:T(128)S(1)} %get-tuple-element.7, bf16[1,128,1152]{2,1,0:T(8,128)(2,1)} %param.7, f32[1152]{0:T(1024)S(1)} %get-tuple-element.10, f32[1152]{0:T(1024)S(1)} %get-tuple-element.11, f32[128]{0:T(128)S(1)} %add_rsqrt_fusion, ...), kind=kOutput, calls=%fused_computation | convolution fusion | flops 95952896 | bytes 1043456 | tf_op jit(solution)/shard_map/dot_general | solution.py:408
  9.9 0.0 copy-start.1
  9.9 121.4 %shard_map.73 = bf16[8,2,20,1152]{3,2,1,0:T(8,128)(2,1)} custom-call(bf16[8,40,1152]{2,1,0:T(8,128)(2,1)} %bitcast.31, bf16[8,288,2304]{2,1,0:T(8,128)(2,1)} %w_in_ref.1, f32[4,1,640]{2,1,0:T(1,128)} %broadcast_in_dim.7.bias_ref, bf16[8,576,1152]{2,1,0:T(8,128)(2,1)} %w_out_ref.1), custom_call_target="tpu_custom_call" | custom-call | tf_op jit(solution)/shard_map/pallas_call | solution.py:416
  131.3 1.3 reshape.71
  132.7 0.4 convolution_multiply_fusion.1
  133.0 0.0 copy-done.1
  133.1 1.1 fusion.4
  (4 shorter events, 0.1 us)
Async XLA Ops:
  0.0 5.8 %copy-start = (bf16[1152,16]{0,1:T(8,128)(2,1)S(1)}, bf16[1152,16]{0,1:T(8,128)(2,1)}, u32[]{:S(2)}) copy-start(bf16[1152,16]{0,1:T(8,128)(2,1)} %param.10) | copy-start | bytes 110596
  9.9 123.1 %copy-start.1 = (bf16[1,128,1152]{2,1,0:T(8,128)(2,1)S(1)}, bf16[1,128,1152]{2,1,0:T(8,128)(2,1)}, u32[]{:S(2)}) copy-start(bf16[1,128,1152]{2,1,0:T(8,128)(2,1)} %param.7) | copy-start | bytes 884740

commit v3 on v2

--- a/solution.py
+++ b/solution.py
@@ -144,40 +144,8 @@
     return result.reshape(1, token_count, width)
 
 
-def one_hot(index, count):
-    return (index[:, None] == jnp.arange(count, dtype=jnp.int32)[None, :]).astype(jnp.bfloat16)
-
-
-def flat_slots(block_ids):
-    flat_ids = block_ids.reshape(-1)
-    pairs = flat_ids.shape[0]
-    hot = one_hot(flat_ids, EXPERTS)
-    order = jnp.arange(pairs, dtype=jnp.int32)
-    before = (order[None, :] < order[:, None]).astype(jnp.bfloat16)
-    earlier = jnp.dot(before, hot, preferred_element_type=jnp.float32)
-    slots = jnp.sum(earlier * hot.astype(jnp.float32), axis=1).astype(jnp.int32)
-    return (flat_ids * CAP + slots).reshape(block_ids.shape)
-
-
-def mixed(tokens, normed, gate_row, router_weight, block_ids, picks, expert_out):
-    logits = jnp.dot(normed, router_weight, preferred_element_type=jnp.float32)
-    chosen = [
-        jnp.sum(
-            jnp.where(block_ids[:, k : k + 1] == jnp.arange(EXPERTS)[None, :], logits, 0.0),
-            axis=1,
-            keepdims=True,
-        )
-        for k in range(2)
-    ]
-    gap = chosen[0] - chosen[1]
-    first = jnp.dot(picks[0], expert_out, preferred_element_type=jnp.float32)
-    second = jnp.dot(picks[1], expert_out, preferred_element_type=jnp.float32)
-    branch = jax.nn.sigmoid(gap) * first + jax.nn.sigmoid(-gap) * second
-    return (tokens.astype(jnp.float32) + gate_row[None, :] * branch).astype(jnp.bfloat16)
-
-
 LANES = 128
-PADDED = 64
+HALF_LANES = 64
 
 
 def flip(index, bit):
@@ -194,13 +162,13 @@
 
 
 def expert_kernel(
-    sizes, send_ref, w_in_ref, bias_ref, w_out_ref, out_ref,
-    got, rows_in, first_w, second_w, acc, r1_out, r1_in, r2_out, r2_in, r3_out,
-    w_send, w_recv, second_sem, t1_send, t1_recv, t2_send, t2_recv,
-    t3_send, t3_recv, t4_send, t4_recv,
+    sizes, hidden_ref, ids_ref, settings_ref, router_ref, w_in_ref, bias_ref, w_out_ref, out_ref,
+    send, got, rows_in, first_w, second_w, acc, r1_out, r1_in, r2_out, r2_in, r3_out, back,
+    w_send, w_recv, second_sem, edge_send, edge_recv,
+    t1_send, t1_recv, t2_send, t2_recv, t3_send, t3_recv, t4_send, t4_recv,
     r1_send, r1_recv, r2_send, r2_recv, r3_send, r3_recv,
 ):
-    parts, members, experts, units, cols, span, depth = sizes
+    parts, members, experts, units, cols, span, depth, pieces = sizes
     group = parts * members
     part, member, shard = (lax.axis_index(n) for n in ("parts", "ep", "fs"))
 
@@ -228,27 +196,70 @@
         )
     pl.semaphore_wait(barrier, len(peers))
 
-    def strip(u, bit):
+    even = shard % 2 == 0
+    rest = span - LANES
+
+    def strip(u, bit, wide):
         target = flipped(shard, bit, 4)
-        start = pl.multiple_of((target * cols) // LANES * LANES, LANES)
-        src = w_in_ref.at[part * units + u, :, pl.ds(start, span)]
-        dst = first_w.at[u, pl.ds(pl.multiple_of(shard * depth, 32), depth), :]
+        start = target // 2 * (2 * cols) + (0 if wide else span)
+        start = pl.multiple_of(start, LANES)
+        src = w_in_ref.at[part * units + u, :, pl.ds(start, span if wide else rest)]
+        rows = pl.ds(pl.multiple_of(shard * depth, 32), depth)
+        dst = first_w.at[u, rows, :] if wide else first_w.at[u, rows, pl.ds(LANES, rest)]
         if bit == 0:
             return pltpu.make_async_copy(src, dst, w_recv.at[u, 0])
         return remote(src, dst, w_send.at[u, bit], w_recv.at[u, bit], shard_peer(bit))
 
-    offset = (shard * cols) % LANES
-
-    def second(u):
-        place = pl.ds(pl.multiple_of(offset, PADDED), cols)
+    def strips_start(u):
+        @pl.when(even)
+        def _():
+            for bit in (2, 3, 1, 0):
+                strip(u, bit, bit % 2 == 0).start()
+
+        @pl.when(shard % 2 == 1)
+        def _():
+            for bit in (2, 3, 1, 0):
+                strip(u, bit, bit % 2 == 1).start()
+
+    def edge(u):
+        return remote(
+            w_out_ref.at[part * units + u, pl.ds(0, HALF_LANES), :],
+            second_w.at[u, pl.ds(cols, HALF_LANES), :],
+            edge_send.at[u], edge_recv.at[u], shard_peer(1),
+        )
+
+    def second_even(u):
         return pltpu.make_async_copy(
-            w_out_ref.at[part * units + u], second_w.at[u, place, :], second_sem.at[u]
-        )
+            w_out_ref.at[part * units + u], second_w.at[u, pl.ds(0, cols), :], second_sem.at[u]
+        )
+
+    def second_odd(u):
+        return pltpu.make_async_copy(
+            w_out_ref.at[part * units + u, pl.ds(HALF_LANES, rest), :],
+            second_w.at[u, pl.ds(LANES, rest), :],
+            second_sem.at[u],
+        )
+
+    def weights_wait(u):
+        @pl.when(even)
+        def _():
+            strip(u, 0, True).wait()
+            for bit in (1, 2, 3):
+                strip(u, bit, True).wait_recv()
+            second_even(u).wait()
+            edge(u).wait_recv()
+
+        @pl.when(shard % 2 == 1)
+        def _():
+            strip(u, 0, False).wait()
+            for bit in (1, 2, 3):
+                strip(u, bit, False).wait_recv()
+            second_odd(u).wait()
 
     def t1(d):
         if d == 0:
-            return pltpu.make_async_copy(send_ref.at[0], got.at[0, 0], t1_recv.at[0])
-        return remote(send_ref.at[d], got.at[0, d], t1_send.at[d], t1_recv.at[d], block_peer(d))
+            return pltpu.make_async_copy(send.at[0], got.at[0, 0], t1_recv.at[0])
+        return remote(send.at[d], got.at[0, d], t1_send.at[d], t1_recv.at[d], block_peer(d))
 
     def t2(d):
         return remote(got.at[0, d], got.at[2, d], t2_send.at[d], t2_recv.at[d], shard_peer(2))
@@ -262,29 +273,73 @@
     def r1(e):
         return remote(r1_out.at[e], r1_in.at[e], r1_send.at[e], r1_recv.at[e], shard_peer(1))
 
-    def r2(e):
-        return remote(r2_out.at[e], r2_in.at[e], r2_send.at[e], r2_recv.at[e], shard_peer(2))
+    def r2(e, i):
+        return remote(
+            r2_out.at[e, i], r2_in.at[e, i], r2_send.at[e, i], r2_recv.at[e, i], shard_peer(2)
+        )
 
     def r3(e, d):
-        src, dst = r3_out.at[e, d], out_ref.at[d, e]
+        src, dst = r3_out.at[e, d], back.at[e, d]
         if d == 0:
             return pltpu.make_async_copy(src, dst, r3_recv.at[e, 0])
         return remote(src, dst, r3_send.at[e, d], r3_recv.at[e, d], block_peer(d))
 
+    early = units // experts
+    for u in range(early):
+        strips_start(u)
+
+    @pl.when(even)
+    def _():
+        for u in range(units):
+            second_even(u).start()
+
+    @pl.when(shard % 2 == 1)
+    def _():
+        for u in range(units):
+            edge(u).start()
+            second_odd(u).start()
+            first_w[u, :, 0:LANES] = jnp.zeros((first_w.shape[1], LANES), first_w.dtype)
+            second_w[u, 0:LANES, :] = jnp.zeros((LANES, second_w.shape[2]), second_w.dtype)
+
+    tokens = hidden_ref[...]
+    count = tokens.shape[0]
+    normed = modulate(tokens, settings_ref[0:1, :], settings_ref[1:2, :])
+    f32, bf16 = jnp.float32, jnp.bfloat16
+    expert_rows = lax.broadcasted_iota(jnp.int32, (EXPERTS, count), 0)
+    ids = [ids_ref[k : k + 1, :] for k in range(2)]
+    hot = [(expert_rows == ids[k]).astype(f32) for k in range(2)]
+    before = (
+        lax.broadcasted_iota(jnp.int32, (count, count), 0)
+        < lax.broadcasted_iota(jnp.int32, (count, count), 1)
+    ).astype(f32)
+    earlier = jnp.dot(
+        (hot[0] + hot[1]).astype(bf16), before.astype(bf16), preferred_element_type=f32
+    )
+    slots = [jnp.sum(earlier * hot[k], axis=0, keepdims=True).astype(jnp.int32) for k in range(2)]
+    own_index = part * members + member
+    holder = [
+        ((i // experts % parts) * members + i // (parts * experts)) ^ own_index for i in ids
+    ]
+    at_holder = [i % experts for i in ids]
+    total_rows = group * experts * CAP
+    place_rows = lax.broadcasted_iota(jnp.int32, (total_rows, count), 0)
+    select = sum(
+        (place_rows == (holder[k] * experts + at_holder[k]) * CAP + slots[k]).astype(f32)
+        for k in range(2)
+    )
+    outgoing = jnp.dot(select.astype(bf16), normed, preferred_element_type=f32).astype(bf16)
+    for d in range(group):
+        send[d] = outgoing[d * experts * CAP : (d + 1) * experts * CAP]
     for d in range(group):
         t1(d).start()
-    early = units // experts
-    for u in range(early):
-        for bit in (2, 3, 1, 0):
-            strip(u, bit).start()
-    if span > cols:
-        spare = (1 - offset // PADDED) * cols
-        for u in range(units):
-            second_w[u, pl.ds(pl.multiple_of(spare, PADDED), span - cols), :] = jnp.zeros(
-                (span - cols, second_w.shape[2]), second_w.dtype
-            )
-    for u in range(units):
-        second(u).start()
+
+    logits = lax.dot_general(
+        router_ref[...], normed, (((1,), (1,)), ((), ())), preferred_element_type=f32
+    )
+    chosen = [jnp.sum(logits * hot[k], axis=0, keepdims=True) for k in range(2)]
+    gap = jnp.broadcast_to(chosen[0] - chosen[1], (count, count)).T[:, 0:1]
+    mix = [jax.nn.sigmoid(gap), jax.nn.sigmoid(-gap)]
+    places = [(at_holder[k] * group + holder[k]) * CAP + slots[k] for k in range(2)]
 
     def arrived(copy, d):
         if d == 0:
@@ -297,8 +352,7 @@
         t2(d).start()
         t3(d).start()
     for u in range(early, units):
-        for bit in (2, 3, 1, 0):
-            strip(u, bit).start()
+        strips_start(u)
     for d in range(group):
         t2(d).wait_recv()
         t4(d).start()
@@ -321,30 +375,43 @@
         t4(d).wait_recv()
     arrange((1, 3), 1)
 
+    piece = half // pieces
+    in_piece = group // pieces
+
     def reply(e):
-        r2(e).wait_recv()
-        total = acc_keep(e) + r2_in[e].astype(jnp.float32)
-        total = total.astype(jnp.bfloat16)
+        for i in range(pieces):
+            r2(e, i).wait_recv()
+            total = acc[e, 0, i * piece : (i + 1) * piece, :] + r2_in[e, i].astype(f32)
+            total = total.astype(bf16)
+            for j in range(in_piece):
+                r3_out[e, i * in_piece + j] = total[j * CAP : (j + 1) * CAP]
+            for j in range(in_piece):
+                r3(e, i * in_piece + j).start()
+
+    def picked(e):
         for d in range(group):
-            r3_out[e, d] = total[d * CAP : (d + 1) * CAP]
-        for d in range(group):
-            r3(e, d).start()
-
-    def acc_keep(e):
-        return acc[e, 0, 0:half, :]
+            arrived(r3(e, d), d)
+        rows = jnp.concatenate([back[e, d] for d in range(group)], axis=0)
+        columns = lax.broadcasted_iota(jnp.int32, (half, count), 0) + e * half
+        branch = 0.0
+        for k in range(2):
+            pick = (columns == places[k]).astype(f32).astype(bf16)
+            branch = branch + mix[k] * lax.dot_general(
+                pick, rows, (((0,), (0,)), ((), ())), preferred_element_type=f32
+            )
+        return branch
 
     for e in range(experts):
         for p in range(SPLIT):
             u = e * SPLIT + p
-            strip(u, 0).wait()
-            for bit in (1, 2, 3):
-                strip(u, bit).wait_recv()
-            second(u).wait()
+            weights_wait(u)
+            start = pl.multiple_of(shard // 2 * (2 * cols) + shard % 2 * (span - LANES), LANES)
+            bias = bias_ref[pl.ds(part * units + u, 1), pl.ds(start, span)]
             for side in (1, 0):
                 pre = jnp.dot(
                     rows_in[e, side], first_w[u], preferred_element_type=jnp.float32
                 )
-                hidden = jax.nn.gelu(pre + bias_ref[u], approximate=True).astype(jnp.bfloat16)
+                hidden = jax.nn.gelu(pre + bias, approximate=True).astype(jnp.bfloat16)
                 made = jnp.dot(hidden, second_w[u], preferred_element_type=jnp.float32)
                 if p > 0:
                     made = made + acc[e, side]
@@ -357,21 +424,36 @@
                 reply(e - 1)
         r1(e).wait_recv()
         chip = acc[e, 0] + r1_in[e].astype(jnp.float32)
-        r2_out[e] = chip[half:].astype(jnp.bfloat16)
-        r2(e).start()
+        for i in range(pieces):
+            r2_out[e, i] = chip[half + i * piece : half + (i + 1) * piece].astype(bf16)
+        for i in range(pieces):
+            r2(e, i).start()
         acc[e, 0] = chip
     reply(experts - 1)
 
+    branch = sum(picked(e) for e in range(experts))
+    out_ref[...] = (tokens.astype(f32) + settings_ref[2:3, :] * branch).astype(bf16)
+
     for e in range(experts):
-        for d in range(group):
-            arrived(r3(e, d), d)
-            if d > 0:
-                r3(e, d).wait_send()
+        for d in range(1, group):
+            r3(e, d).wait_send()
         r1(e).wait_send()
-        r2(e).wait_send()
-    for u in range(units):
-        for bit in (1, 2, 3):
-            strip(u, bit).wait_send()
+        for i in range(pieces):
+            r2(e, i).wait_send()
+
+    @pl.when(even)
+    def _():
+        for u in range(units):
+            for bit in (1, 2, 3):
+                strip(u, bit, bit % 2 == 0).wait_send()
+
+    @pl.when(shard % 2 == 1)
+    def _():
+        for u in range(units):
+            edge(u).wait_send()
+            for bit in (1, 2, 3):
+                strip(u, bit, bit % 2 == 1).wait_send()
+
     for d in range(group):
         if d > 0:
             t1(d).wait_send()
@@ -384,41 +466,25 @@
     token_count = hidden_states.shape[1]
     width = hidden_states.shape[2]
     parts, members, shards = (lax.axis_size(a) for a in ("parts", "ep", "fs"))
-    part, member, shard = (lax.axis_index(a) for a in ("parts", "ep", "fs"))
     group = parts * members
     units = w_in.shape[0] // parts
     experts = units // SPLIT
     depth = w_in.shape[1]
     cols = w_in.shape[2] // shards
     span = cols + cols % LANES
-
-    start = shard * cols // LANES * LANES
-    bias = lax.dynamic_slice(b_in, (part * units, start), (units, span))[:, None, :]
-
-    tokens = hidden_states.reshape(token_count, width)
-    block_ids = expert_ids.reshape(token_count, 2)
-    settings = modulation[0]
-    normed = modulate(tokens, settings[0][None, :], settings[1][None, :])
-    slots = flat_slots(block_ids) - block_ids * CAP
-    holder_member = block_ids // (parts * experts)
-    holder_part = block_ids // experts % parts
-    distance = (holder_part * members + holder_member) ^ (part * members + member)
-    place = (distance * experts + block_ids % experts) * CAP + slots
-    picks = [one_hot(place[:, k], EXPERTS * CAP) for k in range(2)]
-    sending = lax.dot_general(
-        picks[0] + picks[1], normed, (((0,), (0,)), ((), ())), preferred_element_type=jnp.float32
-    ).astype(jnp.bfloat16)
+    pieces = 4 if group % 4 == 0 else 1
 
     rows = 2 * group * CAP
     bf16, dma = jnp.bfloat16, pltpu.SemaphoreType.DMA
     hbm, vmem = pl.BlockSpec(memory_space=pl.ANY), pl.BlockSpec(memory_space=pltpu.VMEM)
-    sizes = (parts, members, experts, units, cols, span, depth)
-    returned = pl.pallas_call(
+    sizes = (parts, members, experts, units, cols, span, depth, pieces)
+    result = pl.pallas_call(
         functools.partial(expert_kernel, sizes),
-        out_shape=jax.ShapeDtypeStruct((group, experts, CAP, width), bf16),
-        in_specs=[hbm, hbm, vmem, hbm],
-        out_specs=hbm,
+        out_shape=jax.ShapeDtypeStruct((token_count, width), bf16),
+        in_specs=[vmem, vmem, vmem, vmem, hbm, vmem, hbm],
+        out_specs=vmem,
         scratch_shapes=[
+            pltpu.VMEM((group, experts * CAP, width), bf16),
             pltpu.VMEM((shards, group, experts * CAP, width), bf16),
             pltpu.VMEM((experts, 2, rows, width), bf16),
             pltpu.VMEM((units, width, span), bf16),
@@ -426,22 +492,28 @@
             pltpu.VMEM((experts, 2, rows, width), jnp.float32),
             pltpu.VMEM((experts, rows, width), bf16),
             pltpu.VMEM((experts, rows, width), bf16),
-            pltpu.VMEM((experts, rows // 2, width), bf16),
-            pltpu.VMEM((experts, rows // 2, width), bf16),
+            pltpu.VMEM((experts, pieces, rows // 2 // pieces, width), bf16),
+            pltpu.VMEM((experts, pieces, rows // 2 // pieces, width), bf16),
+            pltpu.VMEM((experts, group, CAP, width), bf16),
             pltpu.VMEM((experts, group, CAP, width), bf16),
             dma((units, 4)), dma((units, 4)), dma((units,)),
+            dma((units,)), dma((units,)),
         ]
         + [dma((group,))] * 8
-        + [dma((experts,))] * 4
+        + [dma((experts,))] * 2
+        + [dma((experts, pieces))] * 2
         + [dma((experts, group))] * 2,
         compiler_params=pltpu.CompilerParams(
             collective_id=0, has_side_effects=True, vmem_limit_bytes=60 * 1024 * 1024
         ),
-    )(sending.reshape(group, experts * CAP, width), w_in, bias, w_out)
-
-    expert_out = returned.reshape(EXPERTS * CAP, width)
-    result = mixed(
-        tokens, normed, settings[2], router_weight, block_ids, picks, expert_out
+    )(
+        hidden_states.reshape(token_count, width),
+        expert_ids.reshape(token_count, 2).T,
+        modulation[0],
+        router_weight.T,
+        w_in,
+        b_in,
+        w_out,
     )
     return result.reshape(1, token_count, width)
 
@@ -449,7 +521,7 @@
 def solution(mesh):
     sizes = mesh.shape
     group = sizes["ep"] * sizes["parts"]
-    spread = sizes["fs"] == 4 and EXPERTS % group == 0
+    spread = sizes["fs"] == 4 and EXPERTS % group == 0 and sizes["parts"] == 2
     placed = (
         P(("parts", "fs"), "ep", None),
         P(("parts", "fs"), "ep", None),

time: 135 us -> 116 us (0.86)
  Pallas kernels: 121 us -> 113 us
  matrix products: 5.27 us -> 0 us
  other arithmetic: 3.22 us -> 0 us
    pallas_call x1, Pallas kernels: 121 us -> 113 us  [local_spread(): pl.pallas_call(functools.partial(expert_kernel, sizes), out_shape=jax.Sha...]
    dot_general x5 -> x0, matrix products: 5.27 us -> none  [the longest x1 2.32 us: local_spread(): lax.dot_general(picks[0] + picks[1], normed, (((0,), (0,)), ((), ())), pr...]
    reduce_sum x2 -> x0, other arithmetic: 2.28 us -> none  [the longest x1 1.19 us: modulate(): spread = jnp.mean(jnp.square(values - center), axis=-1, keepdims=True)]
    unnamed x5 -> x2, local copies, waits for them, and re-layouts: 0.8 us -> 3.02 us
where the time goes in v3:
time: 116 us
  Pallas kernels  113 us (97%)
  local copies, waits for them, and re-layouts  3.02 us (3%)
    pallas_call x1, Pallas kernels, local_spread(): pl.pallas_call(functools.partial(expert_kernel, sizes), out_shape=jax.Sha...  113 us
    unnamed x2, local copies, waits for them, and re-layouts  3.02 us

profile of v3, /device:TPU:0, one launch (start us, length us, event | category | flops | bytes accessed | tf_op | source)
XLA Modules:
  0.0 115.6 jit_solution(71866445525376292)
XLA Ops:
  0.0 1.3 %copy.10 = f32[1,3,1152]{2,1,0:T(4,128)} copy(f32[1,3,1152]{2,0,1:T(1,128)} %param.9) | data formatting | bytes 27648
  1.3 112.5 %shard_map.73 = bf16[128,1152]{1,0:T(8,128)(2,1)} custom-call(bf16[128,1152]{1,0:T(8,128)(2,1)} %bitcast.10, s32[2,128]{1,0:T(2,128)} %bitcast.13, f32[3,1152]{1,0:T(4,128)} %bitcast.11, bf16[16,1152]{1,0:T(8,128)(2,1)} %bitcast.12, bf16[8,288,2304]{2,1,0:T(8,128)(2,1)} %w_in_ref.1, f32[8,2304]{1,0:T(8,128)} %bias_ref.1, bf16[8,576,1152]{2,1,0:T(8,128)(2,1)} %w_out_ref.1), custom_call_target="tpu_custom_call" | custom-call | tf_op jit(solution)/shard_map/pallas_call | solution.py:481
  113.9 1.7 %copy.12 = bf16[1,128,1152]{2,1,0:T(8,128)(2,1)} copy(bf16[1,128,1152]{2,1,0:T(8,128)(2,1)} %bitcast.9) | data formatting | bytes 589824

commit v4 on v3

--- a/solution.py
+++ b/solution.py
@@ -163,8 +163,8 @@
 
 def expert_kernel(
     sizes, hidden_ref, ids_ref, settings_ref, router_ref, w_in_ref, bias_ref, w_out_ref, out_ref,
-    send, got, rows_in, first_w, second_w, acc, r1_out, r1_in, r2_out, r2_in, r3_out, back,
-    w_send, w_recv, second_sem, edge_send, edge_recv,
+    far_hidden, far_ids, far_settings, send, got, rows_in, first_w, second_w, acc, r1_out, r1_in, r2_out, r2_in, r3_out, back,
+    far_send, far_recv, w_send, w_recv, second_sem, edge_send, edge_recv,
     t1_send, t1_recv, t2_send, t2_recv, t3_send, t3_recv, t4_send, t4_recv,
     r1_send, r1_recv, r2_send, r2_recv, r3_send, r3_recv,
 ):
@@ -256,13 +256,24 @@
                 strip(u, bit, False).wait_recv()
             second_odd(u).wait()
 
+    def far(i):
+        src = (hidden_ref, ids_ref, settings_ref)[i]
+        dst = (far_hidden, far_ids, far_settings)[i]
+        return remote(src, dst, far_send.at[i], far_recv.at[i], shard_peer(2))
+
     def t1(d):
         if d == 0:
-            return pltpu.make_async_copy(send.at[0], got.at[0, 0], t1_recv.at[0])
-        return remote(send.at[d], got.at[0, d], t1_send.at[d], t1_recv.at[d], block_peer(d))
+            return pltpu.make_async_copy(send.at[0, 0], got.at[0, 0], t1_recv.at[0])
+        return remote(
+            send.at[0, d], got.at[0, d], t1_send.at[d], t1_recv.at[d], block_peer(d)
+        )
 
     def t2(d):
-        return remote(got.at[0, d], got.at[2, d], t2_send.at[d], t2_recv.at[d], shard_peer(2))
+        if d == 0:
+            return pltpu.make_async_copy(send.at[1, 0], got.at[2, 0], t2_recv.at[0])
+        return remote(
+            send.at[1, d], got.at[2, d], t2_send.at[d], t2_recv.at[d], block_peer(d)
+        )
 
     def t3(d):
         return remote(got.at[0, d], got.at[1, d], t3_send.at[d], t3_recv.at[d], shard_peer(1))
@@ -284,8 +295,9 @@
             return pltpu.make_async_copy(src, dst, r3_recv.at[e, 0])
         return remote(src, dst, r3_send.at[e, d], r3_recv.at[e, d], block_peer(d))
 
-    early = units // experts
-    for u in range(early):
+    for i in range(3):
+        far(i).start()
+    for u in range(units):
         strips_start(u)
 
     @pl.when(even)
@@ -301,37 +313,47 @@
             first_w[u, :, 0:LANES] = jnp.zeros((first_w.shape[1], LANES), first_w.dtype)
             second_w[u, 0:LANES, :] = jnp.zeros((LANES, second_w.shape[2]), second_w.dtype)
 
+    f32, bf16 = jnp.float32, jnp.bfloat16
     tokens = hidden_ref[...]
     count = tokens.shape[0]
-    normed = modulate(tokens, settings_ref[0:1, :], settings_ref[1:2, :])
-    f32, bf16 = jnp.float32, jnp.bfloat16
     expert_rows = lax.broadcasted_iota(jnp.int32, (EXPERTS, count), 0)
-    ids = [ids_ref[k : k + 1, :] for k in range(2)]
-    hot = [(expert_rows == ids[k]).astype(f32) for k in range(2)]
     before = (
         lax.broadcasted_iota(jnp.int32, (count, count), 0)
         < lax.broadcasted_iota(jnp.int32, (count, count), 1)
-    ).astype(f32)
-    earlier = jnp.dot(
-        (hot[0] + hot[1]).astype(bf16), before.astype(bf16), preferred_element_type=f32
-    )
-    slots = [jnp.sum(earlier * hot[k], axis=0, keepdims=True).astype(jnp.int32) for k in range(2)]
+    ).astype(f32).astype(bf16)
     own_index = part * members + member
-    holder = [
-        ((i // experts % parts) * members + i // (parts * experts)) ^ own_index for i in ids
-    ]
-    at_holder = [i % experts for i in ids]
     total_rows = group * experts * CAP
     place_rows = lax.broadcasted_iota(jnp.int32, (total_rows, count), 0)
-    select = sum(
-        (place_rows == (holder[k] * experts + at_holder[k]) * CAP + slots[k]).astype(f32)
-        for k in range(2)
-    )
-    outgoing = jnp.dot(select.astype(bf16), normed, preferred_element_type=f32).astype(bf16)
-    for d in range(group):
-        send[d] = outgoing[d * experts * CAP : (d + 1) * experts * CAP]
+
+    def dispatch(image, tokens, ids_ref, settings_ref):
+        normed = modulate(tokens, settings_ref[0], settings_ref[1])
+        ids = [ids_ref[k : k + 1, :] for k in range(2)]
+        hot = [(expert_rows == ids[k]).astype(f32) for k in range(2)]
+        earlier = jnp.dot((hot[0] + hot[1]).astype(bf16), before, preferred_element_type=f32)
+        slots = [
+            jnp.sum(earlier * hot[k], axis=0, keepdims=True).astype(jnp.int32) for k in range(2)
+        ]
+        holder = [
+            ((i // experts % parts) * members + i // (parts * experts)) ^ own_index for i in ids
+        ]
+        at_holder = [i % experts for i in ids]
+        select = sum(
+            (place_rows == (holder[k] * experts + at_holder[k]) * CAP + slots[k]).astype(f32)
+            for k in range(2)
+        )
+        outgoing = jnp.dot(select.astype(bf16), normed, preferred_element_type=f32).astype(bf16)
+        for d in range(group):
+            send[image, d] = outgoing[d * experts * CAP : (d + 1) * experts * CAP]
+        return normed, hot, holder, at_holder, slots
+
+    normed, hot, holder, at_holder, slots = dispatch(0, tokens, ids_ref, settings_ref)
     for d in range(group):
         t1(d).start()
+    for i in range(3):
+        far(i).wait_recv()
+    dispatch(1, far_hidden[...], far_ids, far_settings)
+    for d in range(group):
+        t2(d).start()
 
     logits = lax.dot_general(
         router_ref[...], normed, (((1,), (1,)), ((), ())), preferred_element_type=f32
@@ -349,12 +371,9 @@
 
     for d in range(group):
         arrived(t1(d), d)
-        t2(d).start()
         t3(d).start()
-    for u in range(early, units):
-        strips_start(u)
     for d in range(group):
-        t2(d).wait_recv()
+        arrived(t2(d), d)
         t4(d).start()
 
     half = group * CAP
@@ -432,7 +451,7 @@
     reply(experts - 1)
 
     branch = sum(picked(e) for e in range(experts))
-    out_ref[...] = (tokens.astype(f32) + settings_ref[2:3, :] * branch).astype(bf16)
+    out_ref[...] = (tokens.astype(f32) + settings_ref[2] * branch).astype(bf16)
 
     for e in range(experts):
         for d in range(1, group):
@@ -441,6 +460,9 @@
         for i in range(pieces):
             r2(e, i).wait_send()
 
+    for i in range(3):
+        far(i).wait_send()
+
     @pl.when(even)
     def _():
         for u in range(units):
@@ -457,7 +479,7 @@
     for d in range(group):
         if d > 0:
             t1(d).wait_send()
-        t2(d).wait_send()
+            t2(d).wait_send()
         t3(d).wait_send()
         t4(d).wait_send()
 
@@ -484,7 +506,10 @@
         in_specs=[vmem, vmem, vmem, vmem, hbm, vmem, hbm],
         out_specs=vmem,
         scratch_shapes=[
-            pltpu.VMEM((group, experts * CAP, width), bf16),
+            pltpu.VMEM((token_count, width), bf16),
+            pltpu.VMEM((2, token_count), jnp.int32),
+            pltpu.VMEM((modulation.shape[1], 1, width), jnp.float32),
+            pltpu.VMEM((2, group, experts * CAP, width), bf16),
             pltpu.VMEM((shards, group, experts * CAP, width), bf16),
             pltpu.VMEM((experts, 2, rows, width), bf16),
             pltpu.VMEM((units, width, span), bf16),
@@ -496,6 +521,7 @@
             pltpu.VMEM((experts, pieces, rows // 2 // pieces, width), bf16),
             pltpu.VMEM((experts, group, CAP, width), bf16),
             pltpu.VMEM((experts, group, CAP, width), bf16),
+            dma((3,)), dma((3,)),
             dma((units, 4)), dma((units, 4)), dma((units,)),
             dma((units,)), dma((units,)),
         ]
@@ -509,7 +535,7 @@
     )(
         hidden_states.reshape(token_count, width),
         expert_ids.reshape(token_count, 2).T,
-        modulation[0],
+        modulation.transpose(1, 0, 2),
         router_weight.T,
         w_in,
         b_in,

time: 116 us -> 105 us (0.905)
  Pallas kernels: 113 us -> 103 us
  local copies, waits for them, and re-layouts: 3.02 us -> 1.7 us
    pallas_call x1, Pallas kernels: 113 us -> 103 us  [local_spread(): pl.pallas_call(functools.partial(expert_kernel, sizes), out_shape=jax.Sha...]
    unnamed x2 -> x1, local copies, waits for them, and re-layouts: 3.02 us -> 1.7 us
where the time goes in v4:
time: 105 us
  Pallas kernels  103 us (98%)
  local copies, waits for them, and re-layouts  1.7 us (2%)
    pallas_call x1, Pallas kernels, local_spread(): pl.pallas_call(functools.partial(expert_kernel, sizes), out_shape=jax.Sha...  103 us

profile of v4, /device:TPU:0, one launch (start us, length us, event | category | flops | bytes accessed | tf_op | source)
XLA Modules:
  0.0 104.9 jit_solution(2182309099286495381)
XLA Ops:
  0.0 103.2 %shard_map.73 = bf16[128,1152]{1,0:T(8,128)(2,1)} custom-call(bf16[128,1152]{1,0:T(8,128)(2,1)} %bitcast.8, s32[2,128]{1,0:T(2,128)} %bitcast.11, f32[3,1,1152]{2,1,0:T(1,128)} %bitcast.10, bf16[16,1152]{1,0:T(8,128)(2,1)} %bitcast.9, bf16[8,288,2304]{2,1,0:T(8,128)(2,1)} %w_in_ref.1, f32[8,2304]{1,0:T(8,128)} %bias_ref.1, bf16[8,576,1152]{2,1,0:T(8,128)(2,1)} %w_out_ref.1), custom_call_target="tpu_custom_call" | custom-call | tf_op jit(solution)/shard_map/pallas_call | solution.py:503
  103.2 1.7 %copy.9 = bf16[1,128,1152]{2,1,0:T(8,128)(2,1)} copy(bf16[1,128,1152]{2,1,0:T(8,128)(2,1)} %bitcast.7) | data formatting | bytes 589824

commit v5 on v4

--- a/solution.py
+++ b/solution.py
@@ -389,11 +389,6 @@
                     )
 
     arrange((0, 2), 0)
-    for d in range(group):
-        t3(d).wait_recv()
-        t4(d).wait_recv()
-    arrange((1, 3), 1)
-
     piece = half // pieces
     in_piece = group // pieces
 
@@ -426,7 +421,12 @@
             weights_wait(u)
             start = pl.multiple_of(shard // 2 * (2 * cols) + shard % 2 * (span - LANES), LANES)
             bias = bias_ref[pl.ds(part * units + u, 1), pl.ds(start, span)]
-            for side in (1, 0):
+            for side in (1, 0) if p > 0 else (0, 1):
+                if u == 0 and side == 1:
+                    for d in range(group):
+                        t3(d).wait_recv()
+                        t4(d).wait_recv()
+                    arrange((1, 3), 1)
                 pre = jnp.dot(
                     rows_in[e, side], first_w[u], preferred_element_type=jnp.float32
                 )

time: 105 us -> 105 us (level)
  no operation moved by 1% of the time
where the time goes in v5:
time: 105 us
  Pallas kernels  103 us (98%)
  local copies, waits for them, and re-layouts  1.7 us (2%)
    pallas_call x1, Pallas kernels, local_spread(): pl.pallas_call(functools.partial(expert_kernel, sizes), out_shape=jax.Sha...  103 us

profile of v5, /device:TPU:0, one launch (start us, length us, event | category | flops | bytes accessed | tf_op | source)
XLA Modules:
  0.0 105.0 jit_solution(4905240876056479957)
XLA Ops:
  0.0 103.2 %shard_map.73 = bf16[128,1152]{1,0:T(8,128)(2,1)} custom-call(bf16[128,1152]{1,0:T(8,128)(2,1)} %bitcast.8, s32[2,128]{1,0:T(2,128)} %bitcast.11, f32[3,1,1152]{2,1,0:T(1,128)} %bitcast.10, bf16[16,1152]{1,0:T(8,128)(2,1)} %bitcast.9, bf16[8,288,2304]{2,1,0:T(8,128)(2,1)} %w_in_ref.1, f32[8,2304]{1,0:T(8,128)} %bias_ref.1, bf16[8,576,1152]{2,1,0:T(8,128)(2,1)} %w_out_ref.1), custom_call_target="tpu_custom_call" | custom-call | tf_op jit(solution)/shard_map/pallas_call | solution.py:503
  103.3 1.7 %copy.9 = bf16[1,128,1152]{2,1,0:T(8,128)(2,1)} copy(bf16[1,128,1152]{2,1,0:T(8,128)(2,1)} %bitcast.7) | data formatting | bytes 589824
